TPU v7x, 32 devices: a whole 2x2x4 slice. The times are simulated.
32 devices in a mesh: parts: 2 (over y), space: 4 (over z), dp: 2 (over x), chan: 2 (over core).
Axes of the slice: x: 2, y: 2, z: 4, core: 2. Of those that a mesh axis runs over, the one named last changes fastest.
Arguments:
- grad_out: bfloat16 [4, 4, 16, 16, 1024], P(('parts', 'dp'), 'space', None, None, 'chan'), parts along dimension 0, may hold values from -6 to 6
- saved_spectrum: bfloat16 [2, 4, 4, 16, 16, 1024], P(None, ('parts', 'dp'), None, 'space', None, 'chan'), parts along dimension 1, may hold values from -6 to 6
- w_first: bfloat16 [8, 2, 128, 128], P('chan'), may hold values from -0.375 to 0.375
- bias_first: bfloat16 [2, 1024], P(None, 'chan'), may hold values from -3 to 3
- w_second: bfloat16 [8, 2, 128, 128], P('chan'), may hold values from -0.375 to 0.375
Outputs:
- grad_in: bfloat16 [4, 4, 16, 16, 1024], P(('parts', 'dp'), 'space', None, None, 'chan'), parts along dimension 0
- grad_first: float32 [16, 2, 128, 128], P(('parts', 'chan'), None, ('space', 'dp')), parts along dimension 0
- grad_second: float32 [16, 2, 128, 128], P(('parts', 'chan'), None, ('space', 'dp')), parts along dimension 0
There are 2 independent parts, one for each index of `parts`. A program takes and returns all parts, laid end to end along the dimension named above; an argument that names none is the same for every part. Nothing has to cross between parts.
All inputs are finite; a program needn't handle non-finite values.
Results may differ from a plain program's by a relative error of at most 0.013.
Values may be sent and summed in bfloat16 or wider, within the bound.
A program may use at most 64 MiB of HBM per device.

v0:
```python
import math

import jax
import jax.numpy as jnp
from jax import lax
from jax.sharding import PartitionSpec as P

inv_root_two = 1.0 / math.sqrt(2.0)
inv_root_tau = 1.0 / math.sqrt(2.0 * math.pi)
highest = lax.Precision.HIGHEST


def gelu_value(values):
    return values * 0.5 * (1.0 + lax.erf(values * inv_root_two))


def gelu_slope(values):
    return (
        0.5 * (1.0 + lax.erf(values * inv_root_two))
        + values * jnp.exp(-0.5 * values * values) * inv_root_tau
    )


def tables(length, orient):
    position = jnp.arange(length, dtype=jnp.int32)
    phases = position[:, None] * position[None, :] % length
    angles = phases.astype(jnp.float32) * (2.0 * math.pi / length)
    return (jnp.cos(angles), orient * jnp.sin(angles))


def complex_table(length, orient):
    cosine, sine = tables(length, orient)
    return jnp.stack([jnp.stack([cosine, -sine]), jnp.stack([sine, cosine])])


def apply_table(pattern, table, values):
    return jnp.einsum(pattern, table, values, precision=highest, preferred_element_type=jnp.float32)


def forward_product(left, right):
    return jnp.einsum("rbc,bcd->rbd", left, right, preferred_element_type=jnp.float32)


def adjoint_product(left, right):
    return jnp.einsum("rbd,bcd->rbc", left, right, preferred_element_type=jnp.float32)


def weight_product(left, right):
    return jnp.einsum("rbc,rbd->bcd", left, right, preferred_element_type=jnp.float32)


def body(grad_out, saved_spectrum, w_first, bias_first, w_second):
    planes = grad_out.shape[1]
    length_y = grad_out.shape[2]
    length_z = grad_out.shape[3]
    count_local = w_first.shape[0]
    block = w_first.shape[2]
    length_x = planes * lax.axis_size("space")
    cells = length_x * length_y * length_z
    norm_scale = 1.0 / math.sqrt(cells)
    grad_scale = 1.0 / math.sqrt(cells * grad_out.shape[0] * lax.axis_size("dp"))
    source = grad_out.astype(jnp.float32)
    forward_z = jnp.stack(tables(length_z, -1.0))
    partial_spec = apply_table("pkz,sxyzw->psxykw", forward_z, source)
    partial_spec = apply_table("pqky,qsxyzw->psxkzw", complex_table(length_y, -1.0), partial_spec)
    packed = partial_spec.astype(jnp.bfloat16)
    pencil = lax.all_to_all(packed, "space", split_axis=3, concat_axis=2, tiled=True).astype(
        jnp.float32
    )
    spectrum = apply_table("pqkx,qsxyzw->pskyzw", complex_table(length_x, -1.0), pencil)
    grad_pair = (spectrum * norm_scale).astype(jnp.bfloat16)
    pencil_shape = grad_pair.shape[1:]

    def blocks(values):
        return values.reshape(-1, count_local, block)

    grad_real = blocks(grad_pair[0])
    grad_imag = blocks(grad_pair[1])
    saved_real = blocks(saved_spectrum[0])
    saved_imag = blocks(saved_spectrum[1])
    first_real = w_first[:, 0]
    first_imag = w_first[:, 1]
    second_real = w_second[:, 0]
    second_imag = w_second[:, 1]
    bias_real = bias_first[0].astype(jnp.float32).reshape(count_local, block)
    bias_imag = bias_first[1].astype(jnp.float32).reshape(count_local, block)
    pre_real = (
        forward_product(saved_real, first_real)
        - forward_product(saved_imag, first_imag)
        + bias_real
    )
    pre_imag = (
        forward_product(saved_real, first_imag)
        + forward_product(saved_imag, first_real)
        + bias_imag
    )
    act_real = gelu_value(pre_real).astype(jnp.bfloat16)
    act_imag = gelu_value(pre_imag).astype(jnp.bfloat16)
    back_real = adjoint_product(grad_real, second_real) + adjoint_product(grad_imag, second_imag)
    back_imag = adjoint_product(grad_imag, second_real) - adjoint_product(grad_real, second_imag)
    slope_real = (back_real * gelu_slope(pre_real)).astype(jnp.bfloat16)
    slope_imag = (back_imag * gelu_slope(pre_imag)).astype(jnp.bfloat16)
    input_real = adjoint_product(slope_real, first_real) + adjoint_product(slope_imag, first_imag)
    input_imag = adjoint_product(slope_imag, first_real) - adjoint_product(slope_real, first_imag)
    second_term = (
        jnp.stack(
            [
                weight_product(act_real, grad_real) + weight_product(act_imag, grad_imag),
                weight_product(act_real, grad_imag) - weight_product(act_imag, grad_real),
            ],
            axis=1,
        )
        * grad_scale
    )
    first_term = (
        jnp.stack(
            [
                weight_product(saved_real, slope_real) + weight_product(saved_imag, slope_imag),
                weight_product(saved_real, slope_imag) - weight_product(saved_imag, slope_real),
            ],
            axis=1,
        )
        * grad_scale
    )
    input_pair = jnp.stack([input_real.reshape(pencil_shape), input_imag.reshape(pencil_shape)])
    returned = apply_table("pqkx,qsxyzw->pskyzw", complex_table(length_x, 1.0), input_pair).astype(
        jnp.bfloat16
    )
    planes_back = lax.all_to_all(returned, "space", split_axis=2, concat_axis=3, tiled=True).astype(
        jnp.float32
    )
    planes_back = apply_table("pqky,qsxyzw->psxkzw", complex_table(length_y, 1.0), planes_back)
    inverse_cos, inverse_sin = tables(length_z, 1.0)
    inverse_z = jnp.stack([inverse_cos, -inverse_sin])
    field = apply_table("qkz,qsxyzw->sxykw", inverse_z, planes_back)
    grad_in = (field * norm_scale).astype(jnp.bfloat16)
    space_first, space_second = (
        lax.psum_scatter(
            first_term.astype(jnp.bfloat16), "space", scatter_dimension=2, tiled=True
        ).astype(jnp.float32),
        lax.psum_scatter(
            second_term.astype(jnp.bfloat16), "space", scatter_dimension=2, tiled=True
        ).astype(jnp.float32),
    )
    grad_first, grad_second = (
        lax.psum_scatter(
            space_first.astype(jnp.bfloat16), "dp", scatter_dimension=2, tiled=True
        ).astype(jnp.float32),
        lax.psum_scatter(
            space_second.astype(jnp.bfloat16), "dp", scatter_dimension=2, tiled=True
        ).astype(jnp.float32),
    )
    return (grad_in, grad_first, grad_second)


def solution(mesh):
    in_specs = (
        P(("parts", "dp"), "space", None, None, "chan"),
        P(None, ("parts", "dp"), None, "space", None, "chan"),
        P("chan", None, None, None),
        P(None, "chan"),
        P("chan", None, None, None),
    )
    out_specs = (
        P(("parts", "dp"), "space", None, None, "chan"),
        P(("parts", "chan"), None, ("space", "dp"), None),
        P(("parts", "chan"), None, ("space", "dp"), None),
    )
    return jax.shard_map(body, mesh=mesh, in_specs=in_specs, out_specs=out_specs, check_vma=False)
```

profile of v0, /device:TPU:0, one launch (start us, length us, event | category | flops | bytes accessed | tf_op | source)
XLA Modules:
  0.0 124.7 jit_solution(18170415602737115705)
XLA Ops:
  7.4 0.7 copy-done
  8.1 0.5 convolution_bitcast_fusion.4
  8.7 1.7 %fusion.6 = bf16[2,1,1,16,16,512]{5,3,0,4,2,1:T(8,128)(2,1)S(1)} fusion(f32[2,16,16,512,1]{3,2,1,0,4:T(8,128)S(1)} %convolution_bitcast_fusion.4, f32[1,2,16,16]{3,2,1,0:T(8,128)S(1)} %get-tuple-element.26, f32[1,2,16,16]{3,2,1,0:T(8,128)S(1)} %get-tuple-element.25), kind=kOutput, calls=%fused_computation.11 | convolution fusion | flops 100926464 | bytes 1576960 | tf_op jit(solution)/shard_map/pqky,qsxyzw->psxkzw/dot_general | solution.py:37
  10.4 1.4 %copy.147 = bf16[2,1,1,16,16,512]{5,0,4,2,1,3:T(2,128)(2,1)} copy(bf16[2,1,1,16,16,512]{5,3,0,4,2,1:T(8,128)(2,1)S(1)} %fusion.6) | data formatting | bytes 1048576 | tf_op jit(solution)/shard_map/convert_element_type | solution.py:66
  11.7 6.5 %all-to-all-start = ((bf16[2,1,1,16,16,512]{5,0,4,2,1,3:T(2,128)(2,1)}), bf16[2,1,1,16,16,512]{5,0,4,2,1,3:T(2,128)(2,1)S(1)}, u32[]{:S(2)}, u32[]{:S(2)}) async-start(bf16[2,1,1,16,16,512]{5,0,4,2,1,3:T(2,128)(2,1)} %copy.147), calls=%async_computation | async-start | bytes 1048576 | tf_op jit(solution)/shard_map/all_to_all | solution.py:67
  18.5 0.6 copy-done.7
  19.9 1.1 multiply_convert_fusion.1
  21.0 1.1 multiply_convert_fusion
  22.1 10.6 %all-to-all-done = bf16[2,1,1,16,16,512]{5,0,4,2,1,3:T(2,128)(2,1)S(1)} async-done(((bf16[2,1,1,16,16,512]{5,0,4,2,1,3:T(2,128)(2,1)}), bf16[2,1,1,16,16,512]{5,0,4,2,1,3:T(2,128)(2,1)S(1)}, u32[]{:S(2)}, u32[]{:S(2)}) %all-to-all-start) | async-done | bytes 524320 | tf_op jit(solution)/shard_map/all_to_all | solution.py:67
  32.7 1.4 %fusion.4 = bf16[2,1,4,4,16,512]{5,2,0,4,3,1:T(4,128)(2,1)S(1)} fusion(bf16[2,4,4,16,512,1]{4,0,3,2,1,5:T(2,128)(2,1)S(1)} %bitcast.225, f32[1,2,4,4]{3,2,1,0:T(4,128)S(1)} %get-tuple-element.29, f32[1,2,4,4]{3,2,1,0:T(4,128)S(1)} %get-tuple-element.30), kind=kOutput, calls=%fused_computation.9 | convolution fusion | flops 25690176 | bytes 1048832 | tf_op jit(solution)/shard_map/pqkx,qsxyzw->pskyzw/dot_general | solution.py:37
  35.1 0.7 copy-done.4
  36.2 0.8 copy-done.3
  38.5 0.9 copy.201
  39.5 1.4 %fusion.19 = bf16[256,4,128]{2,0,1:T(8,128)(2,1)S(1)} fusion(f32[4,256,128]{2,1,0:T(8,128)S(1)} %fusion.58, f32[256,4,128]{2,0,1:T(8,128)} %get-tuple-element.36, bf16[256,4,128]{2,1,0:T(4,128)(2,1)S(1)} %reshape_squeeze.12, bf16[4,2,128,128]{3,2,1,0:T(8,128)(2,1)S(1)} %copy-done.5), kind=kOutput, calls=%fused_computation.31 | convolution fusion | flops 34996224 | bytes 1703936 | tf_op jit(solution)/shard_map/rbd,bcd->rbc/dot_general | solution.py:45
  41.8 0.9 copy.188
  44.9 0.3 copy.175
  45.2 2.0 %fusion.5 = bf16[2,1,4,4,16,512]{5,2,0,4,3,1:T(4,128)(2,1)S(1)} fusion(f32[1,1,4,4,16,512]{5,2,0,4,3,1:T(4,128)S(1)} %copy.175, f32[1,1,4,4,16,512]{5,2,0,4,3,1:T(4,128)S(1)} %copy.174, f32[1,2,4,4]{3,2,1,0:T(4,128)S(1)} %get-tuple-element.28, f32[1,2,4,4]{3,2,1,0:T(4,128)S(1)} %get-tuple-element.27), kind=kOutput, calls=%fused_computation.10 | convolution fusion | flops 25690176 | bytes 1573120 | tf_op jit(solution)/shard_map/pqkx,qsxyzw->pskyzw/dot_general | solution.py:37
  47.2 1.3 %copy.176 = bf16[2,1,4,4,16,512]{5,0,4,3,1,2:T(2,128)(2,1)} copy(bf16[2,1,4,4,16,512]{5,2,0,4,3,1:T(4,128)(2,1)S(1)} %fusion.5) | data formatting | bytes 1048576 | tf_op jit(solution)/shard_map/convert_element_type | solution.py:126
  48.5 3.5 %all-to-all-start.1 = ((bf16[2,1,4,4,16,512]{5,0,4,3,1,2:T(2,128)(2,1)}), bf16[2,1,4,4,16,512]{5,0,4,3,1,2:T(2,128)(2,1)S(1)}, u32[]{:S(2)}, u32[]{:S(2)}) async-start(bf16[2,1,4,4,16,512]{5,0,4,3,1,2:T(2,128)(2,1)} %copy.176), calls=%async_computation.1 | async-start | bytes 1048576 | tf_op jit(solution)/shard_map/all_to_all | solution.py:129
  52.2 0.6 copy-done.9
  52.9 0.6 dynamic-slice
  54.1 34.1 %all-reduce.9.cloned.1.call-done = (bf16[4,2,128,128]{3,0,1,2:T(4,128)(2,1)}, bf16[4,2,128,128]{3,0,1,2:T(4,128)(2,1)}) async-done(((bf16[4,2,128,128]{3,0,1,2:T(4,128)(2,1)}, bf16[4,2,128,128]{3,0,1,2:T(4,128)(2,1)}), (bf16[4,2,128,128]{3,0,1,2:T(4,128)(2,1)}, bf16[4,2,128,128]{3,0,1,2:T(4,128)(2,1)})) %all-reduce.9.cloned.1.call-update) | async-done | bytes 524304
  88.2 1.5 %constant_dynamic-slice_fusion = bf16[4,2,32,128]{3,0,1,2:T(4,128)(2,1)} fusion(bf16[4,2,128,128]{3,0,1,2:T(4,128)(2,1)} %get-tuple-element.16, u32[]{:T(128)S(6)} %multiply.1), kind=kLoop, calls=%fused_computation.174 | loop fusion | bytes 131076
  89.7 1.5 %constant_dynamic-slice_fusion.1 = bf16[4,2,32,128]{3,0,1,2:T(4,128)(2,1)} fusion(bf16[4,2,128,128]{3,0,1,2:T(4,128)(2,1)} %get-tuple-element.15, u32[]{:T(128)S(6)} %multiply.1), kind=kLoop, calls=%fused_computation.175 | loop fusion | bytes 131076
  91.2 0.6 copy-done.8
  91.8 0.6 dynamic-slice.2
  93.1 19.7 %all-reduce.11.cloned.1.call-done = (bf16[4,2,32,128]{3,0,1,2:T(4,128)(2,1)}, bf16[4,2,32,128]{3,0,1,2:T(4,128)(2,1)}) async-done(((bf16[4,2,32,128]{3,0,1,2:T(4,128)(2,1)}, bf16[4,2,32,128]{3,0,1,2:T(4,128)(2,1)}), (bf16[4,2,32,128]{3,0,1,2:T(4,128)(2,1)}, bf16[4,2,32,128]{3,0,1,2:T(4,128)(2,1)})) %all-reduce.11.cloned.1.call-update) | async-done | bytes 131088
  112.8 0.8 dynamic-slice_convert_fusion
  113.5 0.6 copy.203
  114.4 0.6 copy.202
  115.0 0.8 convolution_bitcast_fusion
  115.8 2.0 %fusion.25 = bf16[1,1,16,16,512]{4,3,2,1,0:T(8,128)(2,1)} fusion(f32[2,16,16,512]{3,1,0,2:T(8,128)S(1)} %convolution_bitcast_fusion, f32[1,16,16]{2,1,0:T(8,128)S(1)} %get-tuple-element.38, f32[1,16,16]{2,1,0:T(8,128)S(1)} %get-tuple-element.40), kind=kOutput, calls=%fused_computation.41 | convolution fusion | flops 50594304 | bytes 1312768 | tf_op jit(solution)/shard_map/qkz,qsxyzw->sxykw/dot_general | solution.py:37
  (61 shorter events, 7.7 us)
Async XLA Ops:
  7.2 1.0 copy-start
  11.7 6.6 %copy-start.2 = (bf16[2,1,4,4,16,512]{5,4,3,2,1,0:T(8,128)(2,1)S(1)}, bf16[2,1,4,4,16,512]{5,4,3,2,1,0:T(8,128)(2,1)}, u32[]{:S(2)}) copy-start(bf16[2,1,4,4,16,512]{5,4,3,2,1,0:T(8,128)(2,1)} %param.6) | copy-start | bytes 1572868
  11.7 21.0 %all-to-all-start = ((bf16[2,1,1,16,16,512]{5,0,4,2,1,3:T(2,128)(2,1)}), bf16[2,1,1,16,16,512]{5,0,4,2,1,3:T(2,128)(2,1)S(1)}, u32[]{:S(2)}, u32[]{:S(2)}) async-start(bf16[2,1,1,16,16,512]{5,0,4,2,1,3:T(2,128)(2,1)} %copy.147), calls=%async_computation | async-start | bytes 1048576 | tf_op jit(solution)/shard_map/all_to_all | solution.py:67
  18.2 70.0 %all-reduce.9.cloned.1.call-start = ((), (), s32[]{:S(2)}) async-start(), calls=%async_computation.2 | async-start | bytes 1048576
  18.4 0.7 copy-start.7
  18.5 1.0 copy-start.1
  34.8 1.0 copy-start.4
  36.0 1.0 copy-start.3
  38.5 1.0 copy-start.5
  48.5 66.6 %all-to-all-start.1 = ((bf16[2,1,4,4,16,512]{5,0,4,3,1,2:T(2,128)(2,1)}), bf16[2,1,4,4,16,512]{5,0,4,3,1,2:T(2,128)(2,1)S(1)}, u32[]{:S(2)}, u32[]{:S(2)}) async-start(bf16[2,1,4,4,16,512]{5,0,4,3,1,2:T(2,128)(2,1)} %copy.176), calls=%async_computation.1 | async-start | bytes 1048576 | tf_op jit(solution)/shard_map/all_to_all | solution.py:129
  52.0 60.8 %all-reduce.11.cloned.1.call-start = ((), (), s32[]{:S(2)}) async-start(), calls=%async_computation.3 | async-start | bytes 262144
  52.2 0.7 copy-start.9
  91.2 0.7 copy-start.8
  113.5 0.8 copy-start.6
Sparse Core Ops, SparseCore 0:
  43.0 45.1 all-reduce.8
  91.3 21.3 all-reduce.10
where the time goes:
time: 125 us
  waiting for transfers between devices  64.4 us (52%)
  local copies, waits for them, and re-layouts  16.8 us (13%)
  matrix products  16.2 us (13%)
  between operations  15.7 us (13%)
  starting transfers between devices  10.2 us (8%)
  other arithmetic  1.25 us (1%)
    unnamed x4, waiting for transfers between devices  53.8 us
    all_to_all x1, waiting for transfers between devices, body(): lax.all_to_all(packed, 'space', split_axis=3, concat_axis=2, tiled=True)  10.6 us
    unnamed x26, local copies, waits for them, and re-layouts  10.1 us
    dot_general x6, matrix products, apply_table(): jnp.einsum(pattern, table, values, precision=highest, preferred_element_t...  8.34 us
    all_to_all x1, starting transfers between devices, body(): lax.all_to_all(packed, 'space', split_axis=3, concat_axis=2, tiled=True)  6.47 us
    all_to_all x1, starting transfers between devices, body(): lax.all_to_all(returned, 'space', split_axis=2, concat_axis=3, tiled=True)  3.47 us
    dot_general x8, matrix products, adjoint_product(): jnp.einsum('rbd,bcd->rbc', left, right, preferred_element_type=jnp.float32)  3.08 us
    dot_general x4, matrix products, forward_product(): jnp.einsum('rbc,bcd->rbd', left, right, preferred_element_type=jnp.float32)  2.6 us
  transfers between devices with their start and end apart: 4, of which 3 were waited for; matrix products, arithmetic and copies ran while one was open for 12% of the time, Pallas kernels for 0%

commit v1 on v0

v1 whole, which is shorter than its diff:
```python
import functools
import math

import jax
import jax.numpy as jnp
import ml_dtypes
import numpy as np
from jax import lax
from jax.experimental import pallas as pl
from jax.experimental.pallas import tpu as pltpu
from jax.sharding import PartitionSpec as P

inv_root_two = 1.0 / math.sqrt(2.0)
inv_root_tau = 1.0 / math.sqrt(2.0 * math.pi)
f32 = jnp.float32
bf16 = jnp.bfloat16
MESH = pl.DeviceIdType.MESH


def scaled_table(table):
    best = None
    for step in range(512):
        factor = 1.0 + step / 512.0
        exact = table * factor
        kept = exact.astype(ml_dtypes.bfloat16).astype(np.float64)
        fit = float((kept * table).sum() / (table * table).sum())
        error = float(((kept - fit * table) ** 2).sum() / (kept**2).sum())
        if best is None or error < best[0]:
            best = (error, fit, kept.astype(ml_dtypes.bfloat16))
    return best[1], best[2]


def plane_table(length_y, length_z, shards):
    ky = np.arange(length_y)[:, None, None, None]
    kz = np.arange(length_z)[None, :, None, None]
    y = np.arange(length_y)[None, None, :, None]
    z = np.arange(length_z)[None, None, None, :]
    angle = 2.0 * np.pi * (ky * y / length_y + kz * z / length_z)
    both = np.stack([np.cos(angle), -np.sin(angle)])
    both = np.round(both, 12)
    both = both.reshape(2, shards, length_y // shards, length_z, length_y * length_z)
    return both.transpose(1, 0, 2, 3, 4).reshape(2 * length_y * length_z, -1)


def times(value, factor):
    re, im = value
    c, s = factor.real, factor.imag
    if abs(s) < 1e-12:
        return (re, im) if abs(c - 1.0) < 1e-12 else (re * c, im * c)
    if abs(c) < 1e-12:
        if abs(s - 1.0) < 1e-12:
            return (-im, re)
        if abs(s + 1.0) < 1e-12:
            return (im, -re)
        return (-im * s, re * s)
    return (re * c - im * s, re * s + im * c)


def plus(a, b):
    return (a[0] + b[0], a[1] + b[1])


def minus(a, b):
    return (a[0] - b[0], a[1] - b[1])


def transform(values, orient):
    n = len(values)
    if n == 1:
        return values
    root = lambda k: complex(math.cos(2 * math.pi * k / n), orient * math.sin(2 * math.pi * k / n))
    if n % 2:
        out = []
        for k in range(n):
            total = values[0]
            for j in range(1, n):
                total = plus(total, times(values[j], root(k * j % n)))
            out.append(total)
        return out
    even = transform(values[0::2], orient)
    odd = transform(values[1::2], orient)
    turned = [times(odd[k], root(k)) for k in range(n // 2)]
    return [plus(even[k], turned[k]) for k in range(n // 2)] + [
        minus(even[k], turned[k]) for k in range(n // 2)
    ]


def dot(a, b, ca, cb):
    return lax.dot_general(a, b, (((ca,), (cb,)), ((), ())), preferred_element_type=f32)


def stacked(re, im):
    top = jnp.concatenate([re, im], axis=1)
    low = jnp.concatenate([-im, re], axis=1)
    return jnp.concatenate([top, low], axis=0)


def kernel(dims, x_hbm, s_hbm, w1_hbm, b_hbm, w2_hbm, t1_hbm, t2_hbm,
           gin_hbm, g1_hbm, g2_hbm,
           x_v, s_v, w1_v, b_v, w2_v, t1_v, t2_v,
           psend, precv, z_v, act, slope, gsc, dz_v, ds_v, qsend, qrecv, gin_v,
           gbuf, drecv, zsend, zrecv, g1_v, g2_v,
           in_sem, out_sem, ps_sem, pr_sem, qs_sem, qr_sem, ds_sem, dr_sem, zs_sem, zr_sem):
    n, m, count, block, length_x, pencil, rows = (
        dims["n"], dims["m"], dims["count"], dims["block"],
        dims["length_x"], dims["pencil"], dims["rows"])
    per = n - 1
    me = lax.axis_index("space")
    mq = lax.axis_index("dp")
    hops = sorted(range(1, n), key=lambda k: abs(k - n / 2))

    loads = [pltpu.make_async_copy(src, dst, in_sem.at[i]) for i, (src, dst) in enumerate(
        [(t1_hbm, t1_v), (x_hbm, x_v), (s_hbm, s_v), (w1_hbm, w1_v), (b_hbm, b_v),
         (w2_hbm, w2_v), (t2_hbm, t2_v)])]
    for load in loads:
        load.start()

    barrier = pltpu.get_barrier_semaphore()
    for k in range(1, n):
        pl.semaphore_signal(barrier, inc=1, device_id={"space": lax.rem(me + k, n)}, device_id_type=MESH)
    for k in range(1, m):
        pl.semaphore_signal(barrier, inc=1, device_id={"dp": lax.rem(mq + k, m)}, device_id_type=MESH)

    loads[0].wait()
    loads[1].wait()
    sends = []
    for b in range(count):
        lanes = slice(b * block, (b + 1) * block)
        psend[b] = dot(t1_v[...], x_v[:, lanes], 1, 0).astype(bf16).reshape(psend.shape[1:])
        if b == 0:
            pl.semaphore_wait(barrier, n - 1 + m - 1)
        for k in hops:
            peer = lax.rem(me + k, n)
            copy = pltpu.make_async_remote_copy(
                src_ref=psend.at[b, peer], dst_ref=precv.at[b, me],
                send_sem=ps_sem.at[b, k - 1], recv_sem=pr_sem.at[b, k - 1],
                device_id={"space": peer}, device_id_type=MESH)
            copy.start()
            sends.append(copy)
        precv[b, me] = psend[b, me]

    loads[2].wait()
    loads[3].wait()
    loads[4].wait()
    bias = b_v[...].astype(f32)
    total = length_x * pencil
    tile = math.gcd(total, 32)
    for b in range(count):
        lanes = slice(b * block, (b + 1) * block)
        w1 = stacked(w1_v[b, 0], w1_v[b, 1])
        pair = jnp.concatenate([s_v[0, :, lanes], s_v[1, :, lanes]], axis=1)
        z_v[...] = dot(pair, w1, 1, 0) + jnp.concatenate([bias[0:1, lanes], bias[1:2, lanes]], axis=1)

        def gelu(t, carry, b=b):
            at = pl.ds(pl.multiple_of(t * tile, tile), tile)
            z = z_v[at, :]
            cdf = 0.5 * (1.0 + lax.erf(z * inv_root_two))
            act[b, at, :] = (z * cdf).astype(bf16)
            slope[b, at, :] = cdf + z * jnp.exp(-0.5 * z * z) * inv_root_tau
            return carry

        lax.fori_loop(0, total // tile, gelu, 0)

    def fold_gradient(b):
        for k in range(1, m):
            drecv_copy(b, k).wait_recv()
        for s in range(n):
            value = gbuf[mq, b, s].astype(f32)
            for k in range(1, m):
                value = value + drecv[k - 1, b, s].astype(f32)
            zsend[b, s] = value.astype(gbuf.dtype)
        for k in hops:
            copy = zsend_copy(b, k)
            copy.start()
            sends.append(copy)

    def drecv_copy(b, k):
        peer = lax.rem(mq + k, m)
        return pltpu.make_async_remote_copy(
            src_ref=gbuf.at[peer, b], dst_ref=drecv.at[k - 1, b],
            send_sem=ds_sem.at[b, k - 1], recv_sem=dr_sem.at[b, k - 1],
            device_id={"dp": peer}, device_id_type=MESH)

    def zsend_copy(b, k):
        peer = lax.rem(me + k, n)
        return pltpu.make_async_remote_copy(
            src_ref=zsend.at[b, peer], dst_ref=zrecv.at[k - 1, b],
            send_sem=zs_sem.at[b, k - 1], recv_sem=zr_sem.at[b, k - 1],
            device_id={"space": peer}, device_id_type=MESH)

    piece = math.gcd(pencil, 16)
    loads[5].wait()
    qcopies = {}
    for b in range(count):
        lanes = slice(b * block, (b + 1) * block)
        for k in range(per):
            sends[b * per + k].wait_recv()
        for r in range(0, pencil, piece):
            planes = [(precv[b, x, r:r + piece, :].astype(f32),
                       precv[b, x, pencil + r:pencil + r + piece, :].astype(f32)) for x in range(length_x)]
            for kx, (re, im) in enumerate(transform(planes, -1.0)):
                at = slice(kx * pencil + r, kx * pencil + r + piece)
                gsc[at, 0:block] = (re * dims["forward_scale"]).astype(bf16)
                gsc[at, block:2 * block] = (im * dims["forward_scale"]).astype(bf16)
        grad = gsc[...]
        w1 = stacked(w1_v[b, 0], w1_v[b, 1])
        w2 = stacked(w2_v[b, 0], w2_v[b, 1])
        dz = (dot(grad, w2, 1, 1) * slope[b]).astype(bf16)
        dz_v[...] = dz
        ds_v[...] = dot(dz, w1, 1, 1)
        for r in range(0, pencil, piece):
            freqs = [(ds_v[kx * pencil + r:kx * pencil + r + piece, 0:block],
                      ds_v[kx * pencil + r:kx * pencil + r + piece, block:2 * block]) for kx in range(length_x)]
            for x, (re, im) in enumerate(transform(freqs, 1.0)):
                qsend[b, x, r:r + piece, :] = re.astype(bf16)
                qsend[b, x, pencil + r:pencil + r + piece, :] = im.astype(bf16)
        for k in hops:
            peer = lax.rem(me + k, n)
            copy = pltpu.make_async_remote_copy(
                src_ref=qsend.at[b, peer], dst_ref=qrecv.at[b, me],
                send_sem=qs_sem.at[b, k - 1], recv_sem=qr_sem.at[b, k - 1],
                device_id={"space": peer}, device_id_type=MESH)
            copy.start()
            qcopies[b, k] = copy
        qrecv[b, me] = qsend[b, me]

        pair = jnp.concatenate([s_v[0, :, lanes], s_v[1, :, lanes]], axis=1)
        for w, (left, right) in enumerate([(pair, dz_v[...]), (act[b], gsc[...])]):
            full = dot(left, right, 0, 0) * dims["grad_scale"]
            real = full[:block, :block] + full[block:, block:]
            imag = full[:block, block:] - full[block:, :block]
            for part, value in enumerate([real, imag]):
                for s in range(n):
                    for q in range(m):
                        at = (s * m + q) * rows
                        gbuf[q, b, s, w, part] = value[at:at + rows].astype(gbuf.dtype)
        for k in range(1, m):
            copy = drecv_copy(b, k)
            copy.start()
            sends.append(copy)
        if b > 0:
            fold_gradient(b - 1)

    fold_gradient(count - 1)
    outs = []
    loads[6].wait()
    for b in range(count):
        lanes = slice(b * block, (b + 1) * block)
        for k in range(1, n):
            qcopies[b, k].wait_recv()
        field = dot(t2_v[...], qrecv[b].reshape(t2_v.shape[1], block), 1, 0)
        gin_v[:, lanes] = (field * dims["inverse_scale"]).astype(bf16)
        copy = pltpu.make_async_copy(gin_v.at[:, lanes], gin_hbm.at[:, lanes], out_sem.at[b])
        copy.start()
        outs.append(copy)
    for b in range(count):
        for k in range(1, n):
            zsend_copy(b, k).wait_recv()
        value = zsend[b, me].astype(f32)
        for k in range(1, n):
            value = value + zrecv[k - 1, b].astype(f32)
        g1_v[b] = value[0]
        g2_v[b] = value[1]
    for i, (src, dst) in enumerate([(g1_v, g1_hbm), (g2_v, g2_hbm)]):
        copy = pltpu.make_async_copy(src, dst, out_sem.at[count + i])
        copy.start()
        outs.append(copy)
    for copy in sends:
        copy.wait_send()
    for copy in qcopies.values():
        copy.wait_send()
    for copy in outs:
        copy.wait()


def body(n, m, grad_out, saved_spectrum, w_first, bias_first, w_second):
    samples, planes, length_y, length_z, width = grad_out.shape
    count, _, block, _ = w_first.shape
    assert samples == 1 and planes == 1
    length_x = planes * n
    cells = length_x * length_y * length_z
    pencil = length_y // n * length_z
    area = length_y * length_z
    total = length_x * pencil
    rows = block // (n * m)
    factor, table = scaled_table(plane_table(length_y, length_z, n))
    norm = 1.0 / math.sqrt(cells)
    dims = dict(n=n, m=m, count=count, block=block, length_x=length_x, pencil=pencil, rows=rows,
                forward_scale=norm / factor, inverse_scale=norm / factor,
                grad_scale=1.0 / math.sqrt(cells * samples * m))
    kept = bf16 if rows % 16 == 0 else f32
    vmem = pltpu.VMEM
    dma = pltpu.SemaphoreType.DMA
    chunk = (2 * pencil, block)
    term = (2, 2, rows, block)
    any_spec = pl.BlockSpec(memory_space=pl.ANY)
    grad_in, grad_first, grad_second = pl.pallas_call(
        functools.partial(kernel, dims),
        out_shape=(
            jax.ShapeDtypeStruct((area, width), bf16),
            jax.ShapeDtypeStruct((count, 2, rows, block), f32),
            jax.ShapeDtypeStruct((count, 2, rows, block), f32),
        ),
        in_specs=[any_spec] * 7,
        out_specs=(any_spec,) * 3,
        scratch_shapes=[
            vmem((area, width), bf16), vmem((2, total, width), bf16), vmem(w_first.shape, bf16),
            vmem(bias_first.shape, bf16), vmem(w_second.shape, bf16),
            vmem(table.shape, bf16), vmem(table.shape[::-1], bf16),
            vmem((count, n) + chunk, bf16), vmem((count, n) + chunk, bf16),
            vmem((total, 2 * block), f32), vmem((count, total, 2 * block), bf16),
            vmem((count, total, 2 * block), f32), vmem((total, 2 * block), bf16),
            vmem((total, 2 * block), bf16), vmem((total, 2 * block), f32),
            vmem((count, n) + chunk, bf16), vmem((count, n) + chunk, bf16), vmem((area, width), bf16),
            vmem((m, count, n) + term, kept), vmem((max(m - 1, 1), count, n) + term, kept),
            vmem((count, n) + term, kept), vmem((max(n - 1, 1), count) + term, kept),
            vmem((count, 2, rows, block), f32), vmem((count, 2, rows, block), f32),
            dma((7,)), dma((count + 2,)),
            dma((count, n)), dma((count, n)), dma((count, n)), dma((count, n)),
            dma((count, m)), dma((count, m)), dma((count, n)), dma((count, n)),
        ],
        compiler_params=pltpu.CompilerParams(collective_id=0, has_side_effects=True),
        name="mixer",
    )(
        grad_out.reshape(area, width), saved_spectrum.reshape(2, total, width), w_first, bias_first, w_second,
        jnp.asarray(table), jnp.asarray(np.ascontiguousarray(table.T)),
    )
    return (grad_in.reshape(grad_out.shape), grad_first, grad_second)


def solution(mesh):
    in_specs = (
        P(("parts", "dp"), "space", None, None, "chan"),
        P(None, ("parts", "dp"), None, "space", None, "chan"),
        P("chan", None, None, None),
        P(None, "chan"),
        P("chan", None, None, None),
    )
    out_specs = (
        P(("parts", "dp"), "space", None, None, "chan"),
        P(("parts", "chan"), None, ("space", "dp"), None),
        P(("parts", "chan"), None, ("space", "dp"), None),
    )
    local = functools.partial(body, mesh.shape["space"], mesh.shape["dp"])
    return jax.shard_map(local, mesh=mesh, in_specs=in_specs, out_specs=out_specs, check_vma=False)
```

time: 125 us -> 39.9 us (0.32)
  waiting for transfers between devices: 64.4 us -> 0 us
  Pallas kernels: 0 us -> 35.8 us
  matrix products: 16.2 us -> 0 us
  between operations: 15.7 us -> 0.65 us
  local copies, waits for them, and re-layouts: 16.8 us -> 3.2 us
  starting transfers between devices: 10.2 us -> 0 us
  other arithmetic: 1.25 us -> 0 us
    unnamed x4 -> x0, waiting for transfers between devices: 53.8 us -> none
    pallas_call x0 -> x1, Pallas kernels: none -> 35.8 us  [body(): pl.pallas_call(functools.partial(kernel, dims), out_shape=(jax.ShapeDtype...]
    dot_general x26 -> x0, matrix products: 16.2 us -> none  [the longest x6 8.34 us: apply_table(): jnp.einsum(pattern, table, values, precision=highest, preferred_element_t...]
    all_to_all x2 -> x0, waiting for transfers between devices: 10.6 us -> none  [the longest x1 10.6 us: body(): lax.all_to_all(packed, 'space', split_axis=3, concat_axis=2, tiled=True)]
    all_to_all x2 -> x0, starting transfers between devices: 9.94 us -> none  [the longest x1 6.47 us: body(): lax.all_to_all(packed, 'space', split_axis=3, concat_axis=2, tiled=True)]
    unnamed x26 -> x7, local copies, waits for them, and re-layouts: 10.1 us -> 3.2 us
    convert_element_type x4 -> x0, local copies, waits for them, and re-layouts: 4.41 us -> none  [the longest x1 1.36 us: body(): packed = partial_spec.astype(jnp.bfloat16)]
    another operation x8 -> x0, local copies, waits for them, and re-layouts: 1.37 us -> none  [the longest x4 1.1 us: body(): jnp.stack([input_real.reshape(pencil_shape), input_imag.reshape(pencil_sh...]
  transfers between devices with their start and end apart: 4 -> 0, of which waited for: 3 -> 0; matrix products, arithmetic and copies ran while one was open for 12% -> 0% of each run, Pallas kernels for 0% -> 0%
where the time goes in v1:
time: 39.9 us; the launch traced here: 39.7 us
  Pallas kernels  35.8 us (90%)
  local copies, waits for them, and re-layouts  3.2 us (8%)
  between operations  0.65 us (2%)
    pallas_call x1, Pallas kernels, body(): pl.pallas_call(functools.partial(kernel, dims), out_shape=(jax.ShapeDtype...  35.8 us
    unnamed x7, local copies, waits for them, and re-layouts  3.2 us

profile of v1, /device:TPU:0, one launch (start us, length us, event | category | flops | bytes accessed | tf_op | source)
XLA Modules:
  0.0 39.7 jit_solution(9329092713296175319)
XLA Ops:
  0.6 35.8 %mixer.1 = (bf16[256,512]{1,0:T(8,128)(2,1)}, f32[4,2,16,128]{3,2,1,0:T(8,128)}, f32[4,2,16,128]{3,2,1,0:T(8,128)}) custom-call(bf16[256,512]{1,0:T(8,128)(2,1)} %bitcast.5, bf16[2,256,512]{2,1,0:T(8,128)(2,1)} %bitcast.3, bf16[4,2,128,128]{3,2,1,0:T(8,128)(2,1)} %w1_hbm.1, bf16[2,512]{1,0:T(2,128)(2,1)} %b_hbm.1, bf16[4,2,128,128]{3,2,1,0:T(8,128)(2,1)} %w2_hbm.1, ...), custom_call_target="tpu_custom_call" | custom-call | tf_op jit(solution)/shard_map/mixer/pallas_call | solution.py:297
  36.5 0.0 copy-start.1
  36.5 1.7 %copy.13 = bf16[1,1,16,16,512]{4,3,2,1,0:T(8,128)(2,1)} copy(bf16[1,1,16,16,512]{4,3,2,1,0:T(8,128)(2,1)} %bitcast.4) | data formatting | bytes 524288
  38.2 0.0 copy-done.1
  38.2 0.0 copy-start
  38.2 0.6 %copy.14 = f32[4,2,16,128]{3,2,1,0:T(8,128)} copy(f32[4,2,16,128]{3,2,1,0:T(8,128)S(1)} %copy-done.1) | data formatting | bytes 131072
  38.8 0.2 copy-done
  39.0 0.6 %copy.15 = f32[4,2,16,128]{3,2,1,0:T(8,128)} copy(f32[4,2,16,128]{3,2,1,0:T(8,128)S(1)} %copy-done) | data formatting | bytes 131072
Async XLA Ops:
  36.5 1.7 %copy-start.1 = (f32[4,2,16,128]{3,2,1,0:T(8,128)S(1)}, f32[4,2,16,128]{3,2,1,0:T(8,128)}, u32[]{:S(2)}) copy-start(f32[4,2,16,128]{3,2,1,0:T(8,128)} %get-tuple-element.13) | copy-start | bytes 196612
  38.2 0.9 %copy-start = (f32[4,2,16,128]{3,2,1,0:T(8,128)S(1)}, f32[4,2,16,128]{3,2,1,0:T(8,128)}, u32[]{:S(2)}) copy-start(f32[4,2,16,128]{3,2,1,0:T(8,128)} %get-tuple-element.14) | copy-start | bytes 196612

commit v2 on v1

--- a/solution.py
+++ b/solution.py
@@ -85,6 +85,10 @@
     ]
 
 
+def reverse(index, bits):
+    return sum(((index >> i) & 1) << (bits - 1 - i) for i in range(bits))
+
+
 def dot(a, b, ca, cb):
     return lax.dot_general(a, b, (((ca,), (cb,)), ((), ())), preferred_element_type=f32)
 
@@ -99,7 +103,7 @@
            gin_hbm, g1_hbm, g2_hbm,
            x_v, s_v, w1_v, b_v, w2_v, t1_v, t2_v,
            psend, precv, z_v, act, slope, gsc, dz_v, ds_v, qsend, qrecv, gin_v,
-           gbuf, drecv, zsend, zrecv, g1_v, g2_v,
+           gbuf, drecv, zbufs, zrecvs, g1_v, g2_v,
            in_sem, out_sem, ps_sem, pr_sem, qs_sem, qr_sem, ds_sem, dr_sem, zs_sem, zr_sem):
     n, m, count, block, length_x, pencil, rows = (
         dims["n"], dims["m"], dims["count"], dims["block"],
@@ -161,18 +165,7 @@
 
         lax.fori_loop(0, total // tile, gelu, 0)
 
-    def fold_gradient(b):
-        for k in range(1, m):
-            drecv_copy(b, k).wait_recv()
-        for s in range(n):
-            value = gbuf[mq, b, s].astype(f32)
-            for k in range(1, m):
-                value = value + drecv[k - 1, b, s].astype(f32)
-            zsend[b, s] = value.astype(gbuf.dtype)
-        for k in hops:
-            copy = zsend_copy(b, k)
-            copy.start()
-            sends.append(copy)
+    levels = len(zbufs) - 1
 
     def drecv_copy(b, k):
         peer = lax.rem(mq + k, m)
@@ -181,12 +174,34 @@
             send_sem=ds_sem.at[b, k - 1], recv_sem=dr_sem.at[b, k - 1],
             device_id={"dp": peer}, device_id_type=MESH)
 
-    def zsend_copy(b, k):
-        peer = lax.rem(me + k, n)
+    def level_copy(b, j):
+        half = n >> (j + 1)
+        bit = lax.rem(me // (1 << j), 2)
         return pltpu.make_async_remote_copy(
-            src_ref=zsend.at[b, peer], dst_ref=zrecv.at[k - 1, b],
-            send_sem=zs_sem.at[b, k - 1], recv_sem=zr_sem.at[b, k - 1],
-            device_id={"space": peer}, device_id_type=MESH)
+            src_ref=zbufs[j].at[b, pl.ds((1 - bit) * half, half)], dst_ref=zrecvs[j].at[b],
+            send_sem=zs_sem.at[b, j], recv_sem=zr_sem.at[b, j],
+            device_id={"space": me + (1 - 2 * bit) * (1 << j)}, device_id_type=MESH)
+
+    def fold_gradient(b, j):
+        if j == 0:
+            for k in range(1, m):
+                drecv_copy(b, k).wait_recv()
+            for s in range(n):
+                value = gbuf[mq, b, s].astype(f32)
+                for k in range(1, m):
+                    value = value + drecv[k - 1, b, s].astype(f32)
+                zbufs[0][b, s] = value.astype(zbufs[0].dtype)
+        else:
+            level_copy(b, j - 1).wait_recv()
+            half = n >> j
+            bit = lax.rem(me // (1 << (j - 1)), 2)
+            for s in range(half):
+                value = zbufs[j - 1][b, bit * half + s].astype(f32) + zrecvs[j - 1][b, s].astype(f32)
+                zbufs[j][b, s] = value.astype(zbufs[j].dtype)
+        if j < levels:
+            copy = level_copy(b, j)
+            copy.start()
+            sends.append(copy)
 
     piece = math.gcd(pencil, 16)
     loads[5].wait()
@@ -233,15 +248,18 @@
                 for s in range(n):
                     for q in range(m):
                         at = (s * m + q) * rows
-                        gbuf[q, b, s, w, part] = value[at:at + rows].astype(gbuf.dtype)
+                        gbuf[q, b, reverse(s, levels), w, part] = value[at:at + rows].astype(gbuf.dtype)
         for k in range(1, m):
             copy = drecv_copy(b, k)
             copy.start()
             sends.append(copy)
-        if b > 0:
-            fold_gradient(b - 1)
-
-    fold_gradient(count - 1)
+        for j in range(min(b, levels)):
+            fold_gradient(b - 1 - j, j)
+
+    for b in range(count, count + levels + 1):
+        for j in range(levels + 1):
+            if 0 <= b - 1 - j < count and j < levels:
+                fold_gradient(b - 1 - j, j)
     outs = []
     loads[6].wait()
     for b in range(count):
@@ -254,13 +272,9 @@
         copy.start()
         outs.append(copy)
     for b in range(count):
-        for k in range(1, n):
-            zsend_copy(b, k).wait_recv()
-        value = zsend[b, me].astype(f32)
-        for k in range(1, n):
-            value = value + zrecv[k - 1, b].astype(f32)
-        g1_v[b] = value[0]
-        g2_v[b] = value[1]
+        fold_gradient(b, levels)
+        g1_v[b] = zbufs[levels][b, 0, 0].astype(f32)
+        g2_v[b] = zbufs[levels][b, 0, 1].astype(f32)
     for i, (src, dst) in enumerate([(g1_v, g1_hbm), (g2_v, g2_hbm)]):
         copy = pltpu.make_async_copy(src, dst, out_sem.at[count + i])
         copy.start()
@@ -288,6 +302,8 @@
     dims = dict(n=n, m=m, count=count, block=block, length_x=length_x, pencil=pencil, rows=rows,
                 forward_scale=norm / factor, inverse_scale=norm / factor,
                 grad_scale=1.0 / math.sqrt(cells * samples * m))
+    levels = n.bit_length() - 1
+    assert n == 1 << levels
     kept = bf16 if rows % 16 == 0 else f32
     vmem = pltpu.VMEM
     dma = pltpu.SemaphoreType.DMA
@@ -313,7 +329,8 @@
             vmem((total, 2 * block), bf16), vmem((total, 2 * block), f32),
             vmem((count, n) + chunk, bf16), vmem((count, n) + chunk, bf16), vmem((area, width), bf16),
             vmem((m, count, n) + term, kept), vmem((max(m - 1, 1), count, n) + term, kept),
-            vmem((count, n) + term, kept), vmem((max(n - 1, 1), count) + term, kept),
+            tuple(vmem((count, n >> j) + term, kept if j < levels else f32) for j in range(levels + 1)),
+            tuple(vmem((count, max(n >> (j + 1), 1)) + term, kept) for j in range(levels)),
             vmem((count, 2, rows, block), f32), vmem((count, 2, rows, block), f32),
             dma((7,)), dma((count + 2,)),
             dma((count, n)), dma((count, n)), dma((count, n)), dma((count, n)),

time: 39.9 us -> 37.4 us (0.937)
  Pallas kernels: 35.8 us -> 33.4 us
    pallas_call x1, Pallas kernels: 35.8 us -> 33.4 us  [body(): pl.pallas_call(functools.partial(kernel, dims), out_shape=(jax.ShapeDtype...]
where the time goes in v2:
time: 37.4 us; the launch traced here: 37.2 us
  Pallas kernels  33.4 us (89%)
  local copies, waits for them, and re-layouts  3.2 us (9%)
  between operations  0.65 us (2%)
    pallas_call x1, Pallas kernels, body(): pl.pallas_call(functools.partial(kernel, dims), out_shape=(jax.ShapeDtype...  33.4 us
    unnamed x7, local copies, waits for them, and re-layouts  3.2 us

profile of v2, /device:TPU:0, one launch (start us, length us, event | category | flops | bytes accessed | tf_op | source)
XLA Modules:
  0.0 37.2 jit_solution(15606702558688646378)
XLA Ops:
  0.6 33.4 %mixer.1 = (bf16[256,512]{1,0:T(8,128)(2,1)}, f32[4,2,16,128]{3,2,1,0:T(8,128)}, f32[4,2,16,128]{3,2,1,0:T(8,128)}) custom-call(bf16[256,512]{1,0:T(8,128)(2,1)} %bitcast.5, bf16[2,256,512]{2,1,0:T(8,128)(2,1)} %bitcast.3, bf16[4,2,128,128]{3,2,1,0:T(8,128)(2,1)} %w1_hbm.1, bf16[2,512]{1,0:T(2,128)(2,1)} %b_hbm.1, bf16[4,2,128,128]{3,2,1,0:T(8,128)(2,1)} %w2_hbm.1, ...), custom_call_target="tpu_custom_call" | custom-call | tf_op jit(solution)/shard_map/mixer/pallas_call | solution.py:313
  34.0 0.0 copy-start.1
  34.0 1.7 %copy.13 = bf16[1,1,16,16,512]{4,3,2,1,0:T(8,128)(2,1)} copy(bf16[1,1,16,16,512]{4,3,2,1,0:T(8,128)(2,1)} %bitcast.4) | data formatting | bytes 524288
  35.7 0.0 copy-done.1
  35.7 0.0 copy-start
  35.7 0.6 %copy.14 = f32[4,2,16,128]{3,2,1,0:T(8,128)} copy(f32[4,2,16,128]{3,2,1,0:T(8,128)S(1)} %copy-done.1) | data formatting | bytes 131072
  36.4 0.2 copy-done
  36.6 0.6 %copy.15 = f32[4,2,16,128]{3,2,1,0:T(8,128)} copy(f32[4,2,16,128]{3,2,1,0:T(8,128)S(1)} %copy-done) | data formatting | bytes 131072
Async XLA Ops:
  34.0 1.7 %copy-start.1 = (f32[4,2,16,128]{3,2,1,0:T(8,128)S(1)}, f32[4,2,16,128]{3,2,1,0:T(8,128)}, u32[]{:S(2)}) copy-start(f32[4,2,16,128]{3,2,1,0:T(8,128)} %get-tuple-element.13) | copy-start | bytes 196612
  35.7 0.9 %copy-start = (f32[4,2,16,128]{3,2,1,0:T(8,128)S(1)}, f32[4,2,16,128]{3,2,1,0:T(8,128)}, u32[]{:S(2)}) copy-start(f32[4,2,16,128]{3,2,1,0:T(8,128)} %get-tuple-element.14) | copy-start | bytes 196612

commit v3 on v2

--- a/solution.py
+++ b/solution.py
@@ -38,8 +38,26 @@
     angle = 2.0 * np.pi * (ky * y / length_y + kz * z / length_z)
     both = np.stack([np.cos(angle), -np.sin(angle)])
     both = np.round(both, 12)
-    both = both.reshape(2, shards, length_y // shards, length_z, length_y * length_z)
-    return both.transpose(1, 0, 2, 3, 4).reshape(2 * length_y * length_z, -1)
+    local = length_y // shards
+    both = both.reshape(2, shards, local, length_z, length_y * length_z).transpose(1, 0, 2, 3, 4)
+    half = length_z // 2
+    chunks = []
+    for d in range(shards):
+        first = both[d, :, 0].reshape(2 * length_z, -1)
+        if d % (shards // 2) == 0:
+            first = np.concatenate([first[: half + 1], first[length_z + 1 : length_z + half], 0 * first[:length_z]])
+        chunks += [both[d, :, 1:].reshape(2 * (local - 1) * length_z, first.shape[1]), first]
+    return np.concatenate(chunks)
+
+
+def mirror_table(length_z):
+    half = length_z // 2
+    out = np.zeros((2 * length_z, length_z))
+    for k in range(length_z):
+        out[k, min(k, length_z - k)] = 1.0
+        if k % half:
+            out[length_z + k, half + min(k, length_z - k)] = 1.0 if k < half else -1.0
+    return out
 
 
 def times(value, factor):
@@ -99,23 +117,52 @@
     return jnp.concatenate([top, low], axis=0)
 
 
-def kernel(dims, x_hbm, s_hbm, w1_hbm, b_hbm, w2_hbm, t1_hbm, t2_hbm,
+def kernel(dims, x_hbm, s_hbm, w1_hbm, b_hbm, w2_hbm, t1_hbm, t2_hbm, mt_hbm,
            gin_hbm, g1_hbm, g2_hbm,
-           x_v, s_v, w1_v, b_v, w2_v, t1_v, t2_v,
+           x_v, s_v, w1_v, b_v, w2_v, t1_v, t2_v, mt_v,
            psend, precv, z_v, act, slope, gsc, dz_v, ds_v, qsend, qrecv, gin_v,
            gbuf, drecv, zbufs, zrecvs, g1_v, g2_v,
            in_sem, out_sem, ps_sem, pr_sem, qs_sem, qr_sem, ds_sem, dr_sem, zs_sem, zr_sem):
     n, m, count, block, length_x, pencil, rows = (
         dims["n"], dims["m"], dims["count"], dims["block"],
         dims["length_x"], dims["pencil"], dims["rows"])
-    per = n - 1
     me = lax.axis_index("space")
     mq = lax.axis_index("dp")
     hops = sorted(range(1, n), key=lambda k: abs(k - n / 2))
 
+    line = dims["line"]
+    full = 2 * pencil
+    short = full - line
+    head = full - 2 * line
+
+    def special(shard):
+        return lax.rem(shard, n // 2) == 0
+
+    def exchange(send, recv, send_sems, recv_sems, b, k, size):
+        peer = lax.rem(me + k, n)
+        return pltpu.make_async_remote_copy(
+            src_ref=send.at[b, peer, 0:size], dst_ref=recv.at[b, me, 0:size],
+            send_sem=send_sems.at[b, k - 1], recv_sem=recv_sems.at[b, k - 1],
+            device_id={"space": peer}, device_id_type=MESH)
+
+    def guarded(mirrored, act_on):
+        @pl.when(mirrored)
+        def _():
+            act_on(short)
+
+        @pl.when(jnp.logical_not(mirrored))
+        def _():
+            act_on(full)
+
+    def first_exchange(b, k, size):
+        return exchange(psend, precv, ps_sem, pr_sem, b, k, size)
+
+    def second_exchange(b, k, size):
+        return exchange(qsend, qrecv, qs_sem, qr_sem, b, k, size)
+
     loads = [pltpu.make_async_copy(src, dst, in_sem.at[i]) for i, (src, dst) in enumerate(
         [(t1_hbm, t1_v), (x_hbm, x_v), (s_hbm, s_v), (w1_hbm, w1_v), (b_hbm, b_v),
-         (w2_hbm, w2_v), (t2_hbm, t2_v)])]
+         (w2_hbm, w2_v), (t2_hbm, t2_v), (mt_hbm, mt_v)])]
     for load in loads:
         load.start()
 
@@ -125,6 +172,9 @@
     for k in range(1, m):
         pl.semaphore_signal(barrier, inc=1, device_id={"dp": lax.rem(mq + k, m)}, device_id_type=MESH)
 
+    for b in range(count):
+        for d in range(0, n, n // 2):
+            qrecv[b, d, short:full, :] = jnp.zeros((line, block), bf16)
     loads[0].wait()
     loads[1].wait()
     sends = []
@@ -134,13 +184,7 @@
         if b == 0:
             pl.semaphore_wait(barrier, n - 1 + m - 1)
         for k in hops:
-            peer = lax.rem(me + k, n)
-            copy = pltpu.make_async_remote_copy(
-                src_ref=psend.at[b, peer], dst_ref=precv.at[b, me],
-                send_sem=ps_sem.at[b, k - 1], recv_sem=pr_sem.at[b, k - 1],
-                device_id={"space": peer}, device_id_type=MESH)
-            copy.start()
-            sends.append(copy)
+            guarded(special(lax.rem(me + k, n)), lambda size: first_exchange(b, k, size).start())
         precv[b, me] = psend[b, me]
 
     loads[2].wait()
@@ -203,18 +247,27 @@
             copy.start()
             sends.append(copy)
 
-    piece = math.gcd(pencil, 16)
+    places = [(head, short)] + [
+        (k * line, head // 2 + k * line) for k in range(pencil // line - 1)]
     loads[5].wait()
-    qcopies = {}
+    loads[7].wait()
     for b in range(count):
         lanes = slice(b * block, (b + 1) * block)
-        for k in range(per):
-            sends[b * per + k].wait_recv()
-        for r in range(0, pencil, piece):
-            planes = [(precv[b, x, r:r + piece, :].astype(f32),
-                       precv[b, x, pencil + r:pencil + r + piece, :].astype(f32)) for x in range(length_x)]
+        for k in range(1, n):
+            guarded(special(me), lambda size: first_exchange(b, k, size).wait_recv())
+
+        @pl.when(special(me))
+        def _():
+            for x in range(length_x):
+                spread = dot(mt_v[...], precv[b, x, head:short, :], 1, 0)
+                precv[b, x, head:full, :] = spread.astype(bf16)
+
+        for r in range(0, pencil, line):
+            re_at, im_at = places[r // line]
+            planes = [(precv[b, x, re_at:re_at + line, :].astype(f32),
+                       precv[b, x, im_at:im_at + line, :].astype(f32)) for x in range(length_x)]
             for kx, (re, im) in enumerate(transform(planes, -1.0)):
-                at = slice(kx * pencil + r, kx * pencil + r + piece)
+                at = slice(kx * pencil + r, kx * pencil + r + line)
                 gsc[at, 0:block] = (re * dims["forward_scale"]).astype(bf16)
                 gsc[at, block:2 * block] = (im * dims["forward_scale"]).astype(bf16)
         grad = gsc[...]
@@ -223,27 +276,29 @@
         dz = (dot(grad, w2, 1, 1) * slope[b]).astype(bf16)
         dz_v[...] = dz
         ds_v[...] = dot(dz, w1, 1, 1)
-        for r in range(0, pencil, piece):
-            freqs = [(ds_v[kx * pencil + r:kx * pencil + r + piece, 0:block],
-                      ds_v[kx * pencil + r:kx * pencil + r + piece, block:2 * block]) for kx in range(length_x)]
+        for r in range(0, pencil, line):
+            re_at, im_at = places[r // line]
+            freqs = [(ds_v[kx * pencil + r:kx * pencil + r + line, 0:block],
+                      ds_v[kx * pencil + r:kx * pencil + r + line, block:2 * block]) for kx in range(length_x)]
             for x, (re, im) in enumerate(transform(freqs, 1.0)):
-                qsend[b, x, r:r + piece, :] = re.astype(bf16)
-                qsend[b, x, pencil + r:pencil + r + piece, :] = im.astype(bf16)
+                qsend[b, x, re_at:re_at + line, :] = re.astype(bf16)
+                qsend[b, x, im_at:im_at + line, :] = im.astype(bf16)
+
+        @pl.when(special(me))
+        def _():
+            for x in range(length_x):
+                merged = dot(mt_v[...], qsend[b, x, head:full, :], 0, 0)
+                qsend[b, x, head:short, :] = merged.astype(bf16)
+
         for k in hops:
-            peer = lax.rem(me + k, n)
-            copy = pltpu.make_async_remote_copy(
-                src_ref=qsend.at[b, peer], dst_ref=qrecv.at[b, me],
-                send_sem=qs_sem.at[b, k - 1], recv_sem=qr_sem.at[b, k - 1],
-                device_id={"space": peer}, device_id_type=MESH)
-            copy.start()
-            qcopies[b, k] = copy
+            guarded(special(me), lambda size: second_exchange(b, k, size).start())
         qrecv[b, me] = qsend[b, me]
 
         pair = jnp.concatenate([s_v[0, :, lanes], s_v[1, :, lanes]], axis=1)
         for w, (left, right) in enumerate([(pair, dz_v[...]), (act[b], gsc[...])]):
-            full = dot(left, right, 0, 0) * dims["grad_scale"]
-            real = full[:block, :block] + full[block:, block:]
-            imag = full[:block, block:] - full[block:, :block]
+            outer = dot(left, right, 0, 0) * dims["grad_scale"]
+            real = outer[:block, :block] + outer[block:, block:]
+            imag = outer[:block, block:] - outer[block:, :block]
             for part, value in enumerate([real, imag]):
                 for s in range(n):
                     for q in range(m):
@@ -265,7 +320,7 @@
     for b in range(count):
         lanes = slice(b * block, (b + 1) * block)
         for k in range(1, n):
-            qcopies[b, k].wait_recv()
+            guarded(special(lax.rem(me + n - k, n)), lambda size: second_exchange(b, k, size).wait_recv())
         field = dot(t2_v[...], qrecv[b].reshape(t2_v.shape[1], block), 1, 0)
         gin_v[:, lanes] = (field * dims["inverse_scale"]).astype(bf16)
         copy = pltpu.make_async_copy(gin_v.at[:, lanes], gin_hbm.at[:, lanes], out_sem.at[b])
@@ -281,8 +336,10 @@
         outs.append(copy)
     for copy in sends:
         copy.wait_send()
-    for copy in qcopies.values():
-        copy.wait_send()
+    for b in range(count):
+        for k in range(1, n):
+            guarded(special(lax.rem(me + k, n)), lambda size: first_exchange(b, k, size).wait_send())
+            guarded(special(me), lambda size: second_exchange(b, k, size).wait_send())
     for copy in outs:
         copy.wait()
 
@@ -299,7 +356,7 @@
     rows = block // (n * m)
     factor, table = scaled_table(plane_table(length_y, length_z, n))
     norm = 1.0 / math.sqrt(cells)
-    dims = dict(n=n, m=m, count=count, block=block, length_x=length_x, pencil=pencil, rows=rows,
+    dims = dict(n=n, m=m, count=count, block=block, length_x=length_x, pencil=pencil, rows=rows, line=length_z,
                 forward_scale=norm / factor, inverse_scale=norm / factor,
                 grad_scale=1.0 / math.sqrt(cells * samples * m))
     levels = n.bit_length() - 1
@@ -317,12 +374,12 @@
             jax.ShapeDtypeStruct((count, 2, rows, block), f32),
             jax.ShapeDtypeStruct((count, 2, rows, block), f32),
         ),
-        in_specs=[any_spec] * 7,
+        in_specs=[any_spec] * 8,
         out_specs=(any_spec,) * 3,
         scratch_shapes=[
             vmem((area, width), bf16), vmem((2, total, width), bf16), vmem(w_first.shape, bf16),
             vmem(bias_first.shape, bf16), vmem(w_second.shape, bf16),
-            vmem(table.shape, bf16), vmem(table.shape[::-1], bf16),
+            vmem(table.shape, bf16), vmem(table.shape[::-1], bf16), vmem((2 * length_z, length_z), bf16),
             vmem((count, n) + chunk, bf16), vmem((count, n) + chunk, bf16),
             vmem((total, 2 * block), f32), vmem((count, total, 2 * block), bf16),
             vmem((count, total, 2 * block), f32), vmem((total, 2 * block), bf16),
@@ -332,7 +389,7 @@
             tuple(vmem((count, n >> j) + term, kept if j < levels else f32) for j in range(levels + 1)),
             tuple(vmem((count, max(n >> (j + 1), 1)) + term, kept) for j in range(levels)),
             vmem((count, 2, rows, block), f32), vmem((count, 2, rows, block), f32),
-            dma((7,)), dma((count + 2,)),
+            dma((8,)), dma((count + 2,)),
             dma((count, n)), dma((count, n)), dma((count, n)), dma((count, n)),
             dma((count, m)), dma((count, m)), dma((count, n)), dma((count, n)),
         ],
@@ -341,7 +398,30 @@
     )(
         grad_out.reshape(area, width), saved_spectrum.reshape(2, total, width), w_first, bias_first, w_second,
         jnp.asarray(table), jnp.asarray(np.ascontiguousarray(table.T)),
+        jnp.asarray(mirror_table(length_z).astype(ml_dtypes.bfloat16)),
     )
+    def place(a, b, c, d, e, f, a_v, b_v, c_v, in_sem, out_sem):
+        quarter = area // 4
+        moves = [(b, b_v, e), (c, c_v, f)] + [
+            (a.at[i * quarter:(i + 1) * quarter], a_v.at[i * quarter:(i + 1) * quarter], d.at[i * quarter:(i + 1) * quarter])
+            for i in range(4)]
+        loads = [pltpu.make_async_copy(x, y, in_sem.at[i]) for i, (x, y, _) in enumerate(moves)]
+        stores = [pltpu.make_async_copy(y, z, out_sem.at[i]) for i, (_, y, z) in enumerate(moves)]
+        for load in loads:
+            load.start()
+        for load, store in zip(loads, stores):
+            load.wait()
+            store.start()
+        for store in stores:
+            store.wait()
+
+    grad_in, grad_first, grad_second = pl.pallas_call(
+        place,
+        out_shape=tuple(jax.ShapeDtypeStruct(a.shape, a.dtype) for a in (grad_in, grad_first, grad_second)),
+        in_specs=[any_spec] * 3, out_specs=(any_spec,) * 3,
+        scratch_shapes=[vmem(a.shape, a.dtype) for a in (grad_in, grad_first, grad_second)] + [dma((6,)), dma((6,))],
+        name="place",
+    )(grad_in, grad_first, grad_second)
     return (grad_in.reshape(grad_out.shape), grad_first, grad_second)
 
 

time: 37.4 us -> 35 us (0.936)
  local copies, waits for them, and re-layouts: 3.2 us -> 0 us
  Pallas kernels: 33.4 us -> 34.2 us
    unnamed x7 -> x0, local copies, waits for them, and re-layouts: 3.2 us -> none
    pallas_call x0 -> x1, Pallas kernels: none -> 1.73 us  [body(): pl.pallas_call(place, out_shape=tuple((jax.ShapeDtypeStruct(a.shape, a.dt...]
    pallas_call x1, Pallas kernels: 33.4 us -> 32.5 us  [body(): pl.pallas_call(functools.partial(kernel, dims), out_shape=(jax.ShapeDtype...]
where the time goes in v3:
time: 35 us; the launch traced here: 34.8 us
  Pallas kernels  34.2 us (98%)
  between operations  0.64 us (2%)
    pallas_call x1, Pallas kernels, body(): pl.pallas_call(functools.partial(kernel, dims), out_shape=(jax.ShapeDtype...  32.5 us
    pallas_call x1, Pallas kernels, body(): pl.pallas_call(place, out_shape=tuple((jax.ShapeDtypeStruct(a.shape, a.dt...  1.73 us

profile of v3, /device:TPU:0, one launch (start us, length us, event | category | flops | bytes accessed | tf_op | source)
XLA Modules:
  0.0 34.8 jit_solution(11465464165528002399)
XLA Ops:
  0.6 32.5 %mixer.1 = (bf16[256,512]{1,0:T(8,128)(2,1)}, f32[4,2,16,128]{3,2,1,0:T(8,128)}, f32[4,2,16,128]{3,2,1,0:T(8,128)}) custom-call(bf16[256,512]{1,0:T(8,128)(2,1)} %bitcast.4, bf16[2,256,512]{2,1,0:T(8,128)(2,1)} %bitcast.3, bf16[4,2,128,128]{3,2,1,0:T(8,128)(2,1)} %w1_hbm.1, bf16[2,512]{1,0:T(2,128)(2,1)} %b_hbm.1, bf16[4,2,128,128]{3,2,1,0:T(8,128)(2,1)} %w2_hbm.1, ...), custom_call_target="tpu_custom_call" | custom-call | tf_op jit(solution)/shard_map/mixer/pallas_call | solution.py:370
  33.1 1.7 %place.1 = (bf16[256,512]{1,0:T(8,128)(2,1)}, f32[4,2,16,128]{3,2,1,0:T(8,128)}, f32[4,2,16,128]{3,2,1,0:T(8,128)}) custom-call(bf16[256,512]{1,0:T(8,128)(2,1)} %get-tuple-element.9.a, f32[4,2,16,128]{3,2,1,0:T(8,128)} %get-tuple-element.10.b, f32[4,2,16,128]{3,2,1,0:T(8,128)} %get-tuple-element.11.c), custom_call_target="tpu_custom_call" | custom-call | tf_op jit(solution)/shard_map/place/pallas_call | solution.py:418

commit v4 on v3

--- a/solution.py
+++ b/solution.py
@@ -163,7 +163,7 @@
     loads = [pltpu.make_async_copy(src, dst, in_sem.at[i]) for i, (src, dst) in enumerate(
         [(t1_hbm, t1_v), (x_hbm, x_v), (s_hbm, s_v), (w1_hbm, w1_v), (b_hbm, b_v),
          (w2_hbm, w2_v), (t2_hbm, t2_v), (mt_hbm, mt_v)])]
-    for load in loads:
+    for load in loads[:2]:
         load.start()
 
     barrier = pltpu.get_barrier_semaphore()
@@ -175,6 +175,8 @@
     for b in range(count):
         for d in range(0, n, n // 2):
             qrecv[b, d, short:full, :] = jnp.zeros((line, block), bf16)
+    for load in loads[2:]:
+        load.start()
     loads[0].wait()
     loads[1].wait()
     sends = []
@@ -193,7 +195,8 @@
     bias = b_v[...].astype(f32)
     total = length_x * pencil
     tile = math.gcd(total, 32)
-    for b in range(count):
+
+    def activate(b):
         lanes = slice(b * block, (b + 1) * block)
         w1 = stacked(w1_v[b, 0], w1_v[b, 1])
         pair = jnp.concatenate([s_v[0, :, lanes], s_v[1, :, lanes]], axis=1)
@@ -251,6 +254,7 @@
         (k * line, head // 2 + k * line) for k in range(pencil // line - 1)]
     loads[5].wait()
     loads[7].wait()
+    activate(0)
     for b in range(count):
         lanes = slice(b * block, (b + 1) * block)
         for k in range(1, n):
@@ -290,10 +294,16 @@
                 merged = dot(mt_v[...], qsend[b, x, head:full, :], 0, 0)
                 qsend[b, x, head:short, :] = merged.astype(bf16)
 
-        for k in hops:
-            guarded(special(me), lambda size: second_exchange(b, k, size).start())
-        qrecv[b, me] = qsend[b, me]
-
+        def pass_on():
+            for k in hops:
+                guarded(special(me), lambda size: second_exchange(b, k, size).start())
+            qrecv[b, me] = qsend[b, me]
+            if b + 1 < count:
+                activate(b + 1)
+
+
+        if b + 1 < count:
+            pass_on()
         pair = jnp.concatenate([s_v[0, :, lanes], s_v[1, :, lanes]], axis=1)
         for w, (left, right) in enumerate([(pair, dz_v[...]), (act[b], gsc[...])]):
             outer = dot(left, right, 0, 0) * dims["grad_scale"]
@@ -308,6 +318,8 @@
             copy = drecv_copy(b, k)
             copy.start()
             sends.append(copy)
+        if b + 1 == count:
+            pass_on()
         for j in range(min(b, levels)):
             fold_gradient(b - 1 - j, j)
 

time: 35 us -> 35 us (level)
  no operation moved by 1% of the time
where the time goes in v4:
time: 35 us; the launch traced here: 34.8 us
  Pallas kernels  34.2 us (98%)
  between operations  0.64 us (2%)
    pallas_call x1, Pallas kernels, body(): pl.pallas_call(functools.partial(kernel, dims), out_shape=(jax.ShapeDtype...  32.4 us
    pallas_call x1, Pallas kernels, body(): pl.pallas_call(place, out_shape=tuple((jax.ShapeDtypeStruct(a.shape, a.dt...  1.73 us

profile of v4, /device:TPU:0, one launch (start us, length us, event | category | flops | bytes accessed | tf_op | source)
XLA Modules:
  0.0 34.8 jit_solution(9744272337913150553)
XLA Ops:
  0.6 32.4 %mixer.1 = (bf16[256,512]{1,0:T(8,128)(2,1)}, f32[4,2,16,128]{3,2,1,0:T(8,128)}, f32[4,2,16,128]{3,2,1,0:T(8,128)}) custom-call(bf16[256,512]{1,0:T(8,128)(2,1)} %bitcast.4, bf16[2,256,512]{2,1,0:T(8,128)(2,1)} %bitcast.3, bf16[4,2,128,128]{3,2,1,0:T(8,128)(2,1)} %w1_hbm.1, bf16[2,512]{1,0:T(2,128)(2,1)} %b_hbm.1, bf16[4,2,128,128]{3,2,1,0:T(8,128)(2,1)} %w2_hbm.1, ...), custom_call_target="tpu_custom_call" | custom-call | tf_op jit(solution)/shard_map/mixer/pallas_call | solution.py:382
  33.1 1.7 %place.1 = (bf16[256,512]{1,0:T(8,128)(2,1)}, f32[4,2,16,128]{3,2,1,0:T(8,128)}, f32[4,2,16,128]{3,2,1,0:T(8,128)}) custom-call(bf16[256,512]{1,0:T(8,128)(2,1)} %get-tuple-element.9.a, f32[4,2,16,128]{3,2,1,0:T(8,128)} %get-tuple-element.10.b, f32[4,2,16,128]{3,2,1,0:T(8,128)} %get-tuple-element.11.c), custom_call_target="tpu_custom_call" | custom-call | tf_op jit(solution)/shard_map/place/pallas_call | solution.py:430
